TPU v7x, 32 devices: a whole 2x2x4 slice. The times are simulated.
32 devices in a mesh: tile: 8 (over y, x, core), chan: 4 (over z).
Axes of the slice: x: 2, y: 2, z: 4, core: 2. Of those that a mesh axis runs over, the one named last changes fastest.
Arguments:
- ensemble: bfloat16 [3072, 128, 256], P('tile', 'chan'), may hold values from -6 to 6
- jacobian: bfloat16 [1280, 128, 128], P('tile', 'chan'), may hold values from -1 to 1
- innovation: float32 [1280, 128], P('tile', 'chan'), may hold values from -6 to 6
- error_vectors: float32 [128, 32], replicated, may hold values from -1 to 1, as said below
- error_values: float32 [128], replicated, may hold values from 0.25 to 4
- ensemble_vectors: float32 [256, 256], replicated, may hold values from -1 to 1, as said below
- column_pick: int32 [8, 5, 40], P('tile'), may hold values from 0 to 383
- footprint_slot: int32 [1280], P('tile'), may hold values from 0 to 199, as said below
- footprint_count: int32 [8], P('tile'), may hold values from 20 to 160, as said below
Outputs:
- analysis: bfloat16 [3072, 128, 256], P('tile', 'chan')
Inputs may be any that keep to these rules, and one draw needn't show every extreme that they name: `footprint_slot`: the 160 entries of one pack are distinct; slot o * 40 + j is the j-th column that tile (pack + 2 - o) mod 8 sends to this pack. `footprint_count`: some pack has all 160 footprints live. `error_vectors`: each block of 32 rows is an orthogonal matrix. `ensemble_vectors`: an orthogonal matrix.
All inputs are finite; a program needn't handle non-finite values.
Results may differ from a plain program's by a relative error of at most 0.013.
Values may be sent and summed in bfloat16 or wider, within the bound.
A program may use at most 64 MiB of HBM per device.

v0:
```python
import jax
import jax.numpy as jnp
from jax import lax
from jax.sharding import PartitionSpec as P


def from_behind(value, axis, steps):
    count = lax.axis_size(axis)
    pairs = [(source, (source + steps) % count) for source in range(count)]
    return lax.ppermute(value, axis, pairs)


def turn_blocks(values, vectors):
    row_count, channels, members = values.shape
    group_width = vectors.shape[1]
    grouped = values.reshape(row_count, channels // group_width, group_width, members)
    basis_blocks = vectors.reshape(channels // group_width, group_width, group_width)
    turned = jnp.einsum("gce,fgck->fgek", basis_blocks, grouped, precision=lax.Precision.HIGHEST)
    return turned.reshape(row_count, channels, members)


def turn_rows(values, vectors):
    row_count, channels = values.shape
    group_width = vectors.shape[1]
    grouped = values.reshape(row_count, channels // group_width, group_width)
    basis_blocks = vectors.reshape(channels // group_width, group_width, group_width)
    turned = jnp.einsum("gce,fgc->fge", basis_blocks, grouped, precision=lax.Precision.HIGHEST)
    return turned.reshape(row_count, channels)


def local(
    ensemble,
    jacobian,
    innovation,
    error_vectors,
    error_values,
    ensemble_vectors,
    column_pick,
    footprint_slot,
    footprint_count,
):
    window = column_pick.shape[1]
    capacity = column_pick.shape[2]
    reach_tiles = window // 2
    level_part = ensemble.shape[1]
    members = ensemble.shape[2]
    chosen = jnp.take(ensemble, column_pick[0].reshape(-1), axis=0).reshape(
        window, capacity, level_part, members
    )
    blocks = []
    for slot_index in range(window):
        shift_by = slot_index - reach_tiles
        if shift_by == 0:
            blocks.append(chosen[slot_index])
        else:
            blocks.append(from_behind(chosen[slot_index], "tile", shift_by))
    arrived = jnp.stack(blocks, 0)
    slot_rows = arrived.reshape(window * capacity, level_part, members)
    columns = jnp.take(slot_rows, footprint_slot, axis=0)
    foot_rows = columns.shape[0]
    live_rows = (jnp.arange(foot_rows, dtype=jnp.int32) < footprint_count[0]).astype(jnp.float32)
    share_rows = foot_rows // lax.axis_size("chan")
    columns, sensitivity, misfit_rows = (
        lax.all_to_all(columns, "chan", split_axis=0, concat_axis=1, tiled=True),
        lax.all_to_all(jacobian, "chan", split_axis=0, concat_axis=1, tiled=True),
        lax.all_to_all(
            innovation.astype(jnp.bfloat16), "chan", split_axis=0, concat_axis=1, tiled=True
        ).astype(innovation.dtype),
    )
    response = jnp.einsum("fcl,flk->fck", sensitivity, columns, preferred_element_type=jnp.float32)
    row_weights = lax.dynamic_slice_in_dim(
        live_rows, lax.axis_index("chan") * share_rows, share_rows, 0
    )
    scales = 1.0 / jnp.sqrt(error_values)
    whitened = (
        turn_blocks(response, error_vectors) * scales[None, :, None] * row_weights[:, None, None]
    )
    misfit = turn_rows(misfit_rows, error_vectors) * scales[None, :]
    pull_sum = jnp.einsum("fck,fc->k", whitened, misfit, precision=lax.Precision.HIGHEST)
    rounded = whitened.astype(jnp.bfloat16).reshape(-1, members)
    gram_sum = lax.dot_general(
        rounded, rounded, (((0,), (0,)), ((), ())), preferred_element_type=jnp.float32
    )
    gram_sum, pull_sum = lax.psum((gram_sum, pull_sum), ("tile", "chan"))
    system = gram_sum + (members - 1) * jnp.eye(members, dtype=jnp.float32)
    factor = jnp.linalg.cholesky(system)
    halfway = lax.linalg.triangular_solve(factor, pull_sum[:, None], left_side=True, lower=True)
    mean_weights = lax.linalg.triangular_solve(
        factor, halfway, left_side=True, lower=True, transpose_a=True
    )[:, 0]
    spread = jnp.sqrt(members - 1.0) * lax.linalg.triangular_solve(
        factor, ensemble_vectors, left_side=True, lower=True, transpose_a=True
    )
    transform = (spread + mean_weights[:, None]).astype(jnp.bfloat16)
    flat_rows = ensemble.reshape(-1, members)
    updated = jnp.dot(flat_rows, transform, preferred_element_type=jnp.float32).astype(jnp.bfloat16)
    return updated.reshape(ensemble.shape)


def solution(mesh):
    return jax.shard_map(
        local,
        mesh=mesh,
        in_specs=(
            P("tile", "chan", None),
            P("tile", "chan", None),
            P("tile", "chan"),
            P(),
            P(),
            P(),
            P("tile", None, None),
            P("tile"),
            P("tile"),
        ),
        out_specs=P("tile", "chan", None),
        check_vma=False,
    )
```

profile of v0, /device:TPU:0, one launch (start us, length us, event | category | flops | bytes accessed | tf_op | source)
XLA Modules:
  0.0 357.7 jit_solution(7432755867193582582)
XLA Ops:
  7.4 5.5 %gather_fusion = bf16[200,32,256]{2,1,0:T(8,128)(2,1)} fusion(bf16[384,32,256]{2,1,0:T(8,128)(2,1)} %param.9, s32[1024]{0:T(1024)S(1)} %pad_clamp_fusion.1), kind=kCustom, calls=%fused_computation | custom fusion | bytes 6554400 | tf_op jit(solution)/shard_map/jit(_take)/gather | solution.py:47
  12.9 2.3 broadcast_select_fusion
  16.8 3.9 %collective-permute-start = (bf16[40,32,256]{2,1,0:T(8,128)(2,1)}, bf16[40,32,256]{2,1,0:T(8,128)(2,1)}, u32[]{:S(2)}, u32[]{:S(2)}) collective-permute-start(bf16[40,32,256]{2,1,0:T(8,128)(2,1)} %get-tuple-element.34), channel_id=1, source_target_pairs={{0,24},{4,28},{8,0},{12,4},{16,8},{20,12},{24,16},{28,20},{1,25},{... | collective-permute-start | bytes 1966088 | tf_op jit(solution)/shard_map/ppermute | solution.py:10
  22.7 4.9 %all-to-all-start.2 = ((bf16[4,2,640]{2,1,0:T(2,128)(2,1)}), bf16[4,2,640]{2,1,0:T(2,128)(2,1)S(1)}, u32[]{:S(2)}, u32[]{:S(2)}) async-start(bf16[4,2,640]{2,1,0:T(2,128)(2,1)} %reshape.193), calls=%async_computation.2 | async-start | bytes 20480 | tf_op jit(solution)/shard_map/all_to_all | solution.py:66
  27.6 5.6 %all-to-all-done.2 = bf16[4,2,640]{2,1,0:T(2,128)(2,1)S(1)} async-done(((bf16[4,2,640]{2,1,0:T(2,128)(2,1)}), bf16[4,2,640]{2,1,0:T(2,128)(2,1)S(1)}, u32[]{:S(2)}, u32[]{:S(2)}) %all-to-all-start.2) | async-done | bytes 10272 | tf_op jit(solution)/shard_map/all_to_all | solution.py:66
  33.2 4.3 %all-to-all-start.1 = ((bf16[160,32,128]{2,1,0:T(8,128)(2,1)}), bf16[160,32,128]{2,1,0:T(8,128)(2,1)}, u32[]{:S(2)}, u32[]{:S(2)}) async-start(bf16[160,32,128]{2,1,0:T(8,128)(2,1)} %param.10), calls=%async_computation.1 | async-start | bytes 2621440 | tf_op jit(solution)/shard_map/all_to_all | solution.py:65
  38.7 11.5 %collective-permute-done.1 = bf16[40,32,256]{2,1,0:T(8,128)(2,1)} collective-permute-done((bf16[40,32,256]{2,1,0:T(8,128)(2,1)}, bf16[40,32,256]{2,1,0:T(8,128)(2,1)}, u32[]{:S(2)}, u32[]{:S(2)}) %collective-permute-start.1) | collective-permute-done | bytes 655392 | tf_op jit(solution)/shard_map/ppermute | solution.py:10
  52.5 11.6 %collective-permute-done.3 = bf16[40,32,256]{2,1,0:T(8,128)(2,1)} collective-permute-done((bf16[40,32,256]{2,1,0:T(8,128)(2,1)}, bf16[40,32,256]{2,1,0:T(8,128)(2,1)}, u32[]{:S(2)}, u32[]{:S(2)}) %collective-permute-start.3) | collective-permute-done | bytes 655392 | tf_op jit(solution)/shard_map/ppermute | solution.py:10
  67.0 2.7 gather_fusion.1
  71.5 5.0 %all-to-all-start = ((bf16[160,32,256]{2,1,0:T(8,128)(2,1)}), bf16[160,32,256]{2,1,0:T(8,128)(2,1)S(1)}, u32[]{:S(2)}, u32[]{:S(2)}) async-start(bf16[160,32,256]{2,1,0:T(8,128)(2,1)} %broadcast_select_fusion.1), calls=%async_computation | async-start | bytes 5242880 | tf_op jit(solution)/shard_map/all_to_all | solution.py:64
  77.9 2.8 copy.24
  80.7 54.4 %all-to-all-done = bf16[160,32,256]{2,1,0:T(8,128)(2,1)S(1)} async-done(((bf16[160,32,256]{2,1,0:T(8,128)(2,1)}), bf16[160,32,256]{2,1,0:T(8,128)(2,1)S(1)}, u32[]{:S(2)}, u32[]{:S(2)}) %all-to-all-start) | async-done | bytes 2621472 | tf_op jit(solution)/shard_map/all_to_all | solution.py:64
  137.3 6.6 %multiply_convert_fusion = (bf16[40,4,32,256]{3,2,0,1:T(8,128)(2,1)S(1)}, f32[40,4,32,256]{3,2,0,1:T(8,128)}) fusion(f32[40]{0:T(128)S(1)} %dynamic_slice.3, f32[4,32]{1,0:T(4,128)S(1)} %mul.53, f32[4,32,32,1]{1,0,2,3:T(4,128)S(1)} %bitcast.144, f32[40,4,32,256]{3,2,1,0:T(8,128)S(1)} %bitcast.138), kind=kOutput, calls=%fused_computation.10 | convolution fusion | flops 507248640 | bytes 13124256 | tf_op jit(solution)/shard_map/gce,fgck->fgek/dot_general | solution.py:18
  145.8 2.9 copy.35
  149.8 2.7 fusion.45
  152.5 37.0 %psum.15 = f32[256]{0:T(256)S(1)} all-reduce(f32[256]{0:T(256)S(1)} %bitcast.148), channel_id=1, replica_groups=mesh['tile'=8,'chan'=4] {'tile','chan'}, use_global_device_ids=true, to_apply=%region_5.6 | all-reduce | flops 256 | bytes 2048 | tf_op jit(solution)/shard_map/psum | solution.py:84
  189.5 81.2 %all-reduce.3.cloned.1.call-done = f32[256,256]{0,1:T(8,128)} async-done(((f32[256,256]{0,1:T(8,128)}), f32[256,256]{0,1:T(8,128)}) %all-reduce.3.cloned.1.call-update) | async-done | bytes 262160 | tf_op jit(solution)/shard_map/psum | solution.py:84
  272.8 11.7 %cholesky.49 = f32[128,128]{1,0:T(8,128)S(1)} custom-call(f32[128,128]{1,0:T(8,128)S(1)} %cholesky.115), custom_call_target="Cholesky" | custom-call | tf_op jit(solution)/shard_map/jit(cholesky)/cholesky | solution.py:86
  284.5 9.8 %custom-call.18 = f32[1,128,128]{1,2,0:T(8,128)S(1)} custom-call(f32[1,128,128]{2,1,0:T(8,128)S(1)} %get-tuple-element.36), custom_call_target="InvertDiagBlocksLowerTriangular" | custom-call | tf_op jit(solution)/shard_map/jit(cholesky)/cholesky | solution.py:86
  294.8 11.7 %cholesky.103 = f32[128,128]{1,0:T(8,128)S(1)} custom-call(f32[128,128]{1,0:T(8,128)S(1)} %convolution_subtract_fusion.1), custom_call_target="Cholesky" | custom-call | tf_op jit(solution)/shard_map/jit(cholesky)/cholesky | solution.py:86
  308.9 4.0 %while.1 = (s32[]{:T(128)}, f32[256,256]{0,1:T(8,128)S(1)}, s32[2,2]{1,0:T(2,128)S(1)}, f32[2,128,128]{2,1,0:T(8,128)S(1)}, s32[]{:T(128)}) while((s32[]{:T(128)}, f32[256,256]{0,1:T(8,128)S(1)}, s32[2,2]{1,0:T(2,128)S(1)}, f32[2,128,128]{2,1,0:T(8,128)S(1)}, s32[]{:T(128)}) %tuple.27), condition=%wide.while_cond, body=%wide.while_body.sunk | while | flops 2 | bytes 393321 | solution.py:91
  312.9 19.9 %custom-call.19 = f32[2,128,128]{1,2,0:T(8,128)S(1)} custom-call(f32[2,128,128]{2,1,0:T(8,128)S(1)} %get-tuple-element.12), custom_call_target="InvertDiagBlocksLowerTriangular" | custom-call | tf_op jit(solution)/shard_map/triangular_solve | solution.py:91
  334.9 7.4 %fusion = bf16[12288,256]{0,1:T(8,128)(2,1)} fusion(bf16[12288,256]{1,0:T(8,128)(2,1)} %bitcast.139, f32[128,256]{1,0:T(8,128)S(1)} %fusion.23, f32[128,256]{1,0:T(8,128)S(1)} %fusion.32, f32[256]{0:T(256)S(1)} %bitcast.147), kind=kOutput, calls=%fused_computation.5 | convolution fusion | flops 1614020608 | bytes 12846080 | tf_op jit(solution)/shard_map/dot_general | solution.py:96
  342.3 8.6 %copy.38 = bf16[12288,256]{1,0:T(8,128)(2,1)} copy(bf16[12288,256]{0,1:T(8,128)(2,1)} %fusion) | data formatting | bytes 12582912 | tf_op jit(solution)/shard_map/convert_element_type | solution.py:96
  (94 shorter events, 27.9 us)
Async XLA Ops:
  15.2 6.7 %copy-start.3 = (f32[160,32]{0,1:T(8,128)S(1)}, f32[160,32]{0,1:T(8,128)}, u32[]{:S(2)}) copy-start(f32[160,32]{0,1:T(8,128)} %param.11) | copy-start | bytes 61444
  15.3 12.4 %copy-start.5 = (s32[160]{0:T(256)S(1)}, s32[160]{0:T(256)}, u32[]{:S(2)}) copy-start(s32[160]{0:T(256)} %param.16) | copy-start | bytes 1924
  16.8 20.7 %collective-permute-start = (bf16[40,32,256]{2,1,0:T(8,128)(2,1)}, bf16[40,32,256]{2,1,0:T(8,128)(2,1)}, u32[]{:S(2)}, u32[]{:S(2)}) collective-permute-start(bf16[40,32,256]{2,1,0:T(8,128)(2,1)} %get-tuple-element.34), channel_id=1, source_target_pairs={{0,24},{4,28},{8,0},{12,4},{16,8},{20,12},{24,16},{28,20},{1,25},{... | collective-permute-start | bytes 1966088 | tf_op jit(solution)/shard_map/ppermute | solution.py:10
  20.7 29.5 %collective-permute-start.1 = (bf16[40,32,256]{2,1,0:T(8,128)(2,1)}, bf16[40,32,256]{2,1,0:T(8,128)(2,1)}, u32[]{:S(2)}, u32[]{:S(2)}) collective-permute-start(bf16[40,32,256]{2,1,0:T(8,128)(2,1)} %get-tuple-element.33), channel_id=1, source_target_pairs={{0,28},{4,0},{8,4},{12,8},{16,12},{20,16},{24,20},{28,24},{1,29},{... | collective-permute-start | bytes 1966088 | tf_op jit(solution)/shard_map/ppermute | solution.py:10
  20.7 30.7 %collective-permute-start.2 = (bf16[40,32,256]{2,1,0:T(8,128)(2,1)}, bf16[40,32,256]{2,1,0:T(8,128)(2,1)}, u32[]{:S(2)}, u32[]{:S(2)}) collective-permute-start(bf16[40,32,256]{2,1,0:T(8,128)(2,1)} %get-tuple-element.32), channel_id=1, source_target_pairs={{0,4},{4,8},{8,12},{12,16},{16,20},{20,24},{24,28},{28,0},{1,5},{5... | collective-permute-start | bytes 1966088 | tf_op jit(solution)/shard_map/ppermute | solution.py:10
  21.2 42.9 %collective-permute-start.3 = (bf16[40,32,256]{2,1,0:T(8,128)(2,1)}, bf16[40,32,256]{2,1,0:T(8,128)(2,1)}, u32[]{:S(2)}, u32[]{:S(2)}) collective-permute-start(bf16[40,32,256]{2,1,0:T(8,128)(2,1)} %get-tuple-element.31), channel_id=1, source_target_pairs={{0,8},{4,12},{8,16},{12,20},{16,24},{20,28},{24,0},{28,4},{1,9},{5... | collective-permute-start | bytes 1966088 | tf_op jit(solution)/shard_map/ppermute | solution.py:10
  22.7 10.5 %all-to-all-start.2 = ((bf16[4,2,640]{2,1,0:T(2,128)(2,1)}), bf16[4,2,640]{2,1,0:T(2,128)(2,1)S(1)}, u32[]{:S(2)}, u32[]{:S(2)}) async-start(bf16[4,2,640]{2,1,0:T(2,128)(2,1)} %reshape.193), calls=%async_computation.2 | async-start | bytes 20480 | tf_op jit(solution)/shard_map/all_to_all | solution.py:66
  33.2 38.3 %all-to-all-start.1 = ((bf16[160,32,128]{2,1,0:T(8,128)(2,1)}), bf16[160,32,128]{2,1,0:T(8,128)(2,1)}, u32[]{:S(2)}, u32[]{:S(2)}) async-start(bf16[160,32,128]{2,1,0:T(8,128)(2,1)} %param.10), calls=%async_computation.1 | async-start | bytes 2621440 | tf_op jit(solution)/shard_map/all_to_all | solution.py:65
  65.2 1.7 copy-start.1
  71.5 5.7 %copy-start.6 = (f32[128]{0:T(128)S(1)}, f32[128]{0:T(128)}, u32[]{:S(2)}) copy-start(f32[128]{0:T(128)} %param.13) | copy-start | bytes 1540
  71.5 5.8 %copy-start.4 = (f32[128,32]{0,1:T(8,128)S(1)}, f32[128,32]{0,1:T(8,128)}, u32[]{:S(2)}) copy-start(f32[128,32]{0,1:T(8,128)} %param.12) | copy-start | bytes 49156
  71.5 63.6 %all-to-all-start = ((bf16[160,32,256]{2,1,0:T(8,128)(2,1)}), bf16[160,32,256]{2,1,0:T(8,128)(2,1)S(1)}, u32[]{:S(2)}, u32[]{:S(2)}) async-start(bf16[160,32,256]{2,1,0:T(8,128)(2,1)} %broadcast_select_fusion.1), calls=%async_computation | async-start | bytes 5242880 | tf_op jit(solution)/shard_map/all_to_all | solution.py:64
  76.5 194.1 %all-reduce.3.cloned.1.call-start = ((), (), s32[]{:S(2)}) async-start(), calls=%async_computation.3 | async-start | bytes 524288 | tf_op jit(solution)/shard_map/psum | solution.py:84
  135.1 1.3 copy-start
  189.5 144.6 %copy-start.2 = (f32[256,256]{1,0:T(8,128)S(1)}, f32[256,256]{1,0:T(8,128)}, u32[]{:S(2)}) copy-start(f32[256,256]{1,0:T(8,128)} %param.14) | copy-start | bytes 786436
Sparse Core Ops, SparseCore 0:
  145.9 124.6 all-reduce.2
where the time goes:
time: 359 us; the launch traced here: 358 us
  waiting for transfers between devices  164 us (46%)
  other arithmetic  61.9 us (17%)
  local copies, waits for them, and re-layouts  37.6 us (10%)
  blocking collectives  37 us (10%)
  matrix products  21.9 us (6%)
  starting transfers between devices  19.3 us (5%)
  between operations  15.6 us (4%)
    psum x1, waiting for transfers between devices, local(): gram_sum, pull_sum = lax.psum((gram_sum, pull_sum), ('tile', 'chan'))  81.2 us
    all_to_all x1, waiting for transfers between devices, local(): lax.all_to_all(columns, 'chan', split_axis=0, concat_axis=1, tiled=True)  54.4 us
    psum x1, blocking collectives, local(): gram_sum, pull_sum = lax.psum((gram_sum, pull_sum), ('tile', 'chan'))  37 us
    another operation x6, other arithmetic, local(): factor = jnp.linalg.cholesky(system)  33.9 us
    ppermute x4, waiting for transfers between devices, from_behind(): return lax.ppermute(value, axis, pairs)  23.1 us
    another operation x3, other arithmetic, local(): lax.linalg.triangular_solve(factor, ensemble_vectors, left_side=True, low...  20 us
    convert_element_type x1, local copies, waits for them, and re-layouts, local(): jnp.dot(flat_rows, transform, preferred_element_type=jnp.float32)  8.6 us
    dot_general x1, matrix products, local(): jnp.dot(flat_rows, transform, preferred_element_type=jnp.float32)  7.38 us
  transfers between devices with their start and end apart: 8, of which 5 were waited for; matrix products, arithmetic and copies ran while one was open for 6% of the time, Pallas kernels for 0%

commit v1 on v0

--- a/solution.py
+++ b/solution.py
@@ -2,6 +2,7 @@
 import jax.numpy as jnp
 from jax import lax
 from jax.sharding import PartitionSpec as P
+from jax.lax import psum
 
 
 def from_behind(value, axis, steps):
@@ -81,7 +82,8 @@
     gram_sum = lax.dot_general(
         rounded, rounded, (((0,), (0,)), ((), ())), preferred_element_type=jnp.float32
     )
-    gram_sum, pull_sum = lax.psum((gram_sum, pull_sum), ("tile", "chan"))
+    rest_packet_over_axis = lambda matrix: psum(psum(matrix, "tile"), "chan")
+    gram_sum, pull_sum = rest_packet_over_axis((gram_sum, pull_sum))
     system = gram_sum + (members - 1) * jnp.eye(members, dtype=jnp.float32)
     factor = jnp.linalg.cholesky(system)
     halfway = lax.linalg.triangular_solve(factor, pull_sum[:, None], left_side=True, lower=True)

time: 359 us -> 324 us (0.903)
  waiting for transfers between devices: 164 us -> 137 us
  blocking collectives: 37 us -> 24 us
    psum x1 -> x2, waiting for transfers between devices: 81.2 us -> 54.2 us  [local(): rest_packet_over_axis = lambda matrix: psum(psum(matrix, 'tile'), 'chan')]
    psum x1 -> x2, blocking collectives: 37 us -> 24 us  [local(): rest_packet_over_axis = lambda matrix: psum(psum(matrix, 'tile'), 'chan')]
  transfers between devices with their start and end apart: 8 -> 9, of which waited for: 5 -> 6; matrix products, arithmetic and copies ran while one was open for 6% -> 8% of each run, Pallas kernels for 0% -> 0%
where the time goes in v1:
time: 324 us; the launch traced here: 323 us
  waiting for transfers between devices  137 us (42%)
  other arithmetic  64.6 us (20%)
  local copies, waits for them, and re-layouts  37.8 us (12%)
  blocking collectives  24 us (7%)
  matrix products  23.7 us (7%)
  starting transfers between devices  19.3 us (6%)
  between operations  15.7 us (5%)
    all_to_all x1, waiting for transfers between devices, local(): lax.all_to_all(columns, 'chan', split_axis=0, concat_axis=1, tiled=True)  54.4 us
    psum x2, waiting for transfers between devices, local(): rest_packet_over_axis = lambda matrix: psum(psum(matrix, 'tile'), 'chan')  54.2 us
    another operation x6, other arithmetic, local(): factor = jnp.linalg.cholesky(system)  34 us
    psum x2, blocking collectives, local(): rest_packet_over_axis = lambda matrix: psum(psum(matrix, 'tile'), 'chan')  24 us
    ppermute x4, waiting for transfers between devices, from_behind(): return lax.ppermute(value, axis, pairs)  23.1 us
    another operation x3, other arithmetic, local(): lax.linalg.triangular_solve(factor, ensemble_vectors, left_side=True, low...  19.9 us
    convert_element_type x1, local copies, waits for them, and re-layouts, local(): jnp.dot(flat_rows, transform, preferred_element_type=jnp.float32)  8.6 us
    dot_general x1, matrix products, local(): jnp.dot(flat_rows, transform, preferred_element_type=jnp.float32)  7.38 us
  transfers between devices with their start and end apart: 9, of which 6 were waited for; matrix products, arithmetic and copies ran while one was open for 8% of the time, Pallas kernels for 0%

profile of v1, /device:TPU:0, one launch (start us, length us, event | category | flops | bytes accessed | tf_op | source)
XLA Modules:
  0.0 322.5 jit_solution(14947929338174270441)
XLA Ops:
  7.4 5.5 %gather_fusion = bf16[200,32,256]{2,1,0:T(8,128)(2,1)} fusion(bf16[384,32,256]{2,1,0:T(8,128)(2,1)} %param.9, s32[1024]{0:T(1024)S(1)} %pad_clamp_fusion.1), kind=kCustom, calls=%fused_computation | custom fusion | bytes 6554400 | tf_op jit(solution)/shard_map/jit(_take)/gather | solution.py:48
  16.8 3.9 %collective-permute-start = (bf16[40,32,256]{2,1,0:T(8,128)(2,1)}, bf16[40,32,256]{2,1,0:T(8,128)(2,1)}, u32[]{:S(2)}, u32[]{:S(2)}) collective-permute-start(bf16[40,32,256]{2,1,0:T(8,128)(2,1)} %get-tuple-element.34), channel_id=1, source_target_pairs={{0,24},{4,28},{8,0},{12,4},{16,8},{20,12},{24,16},{28,20},{1,25},{... | collective-permute-start | bytes 1966088 | tf_op jit(solution)/shard_map/ppermute | solution.py:11
  22.7 4.9 %all-to-all-start.2 = ((bf16[4,2,640]{2,1,0:T(2,128)(2,1)}), bf16[4,2,640]{2,1,0:T(2,128)(2,1)S(1)}, u32[]{:S(2)}, u32[]{:S(2)}) async-start(bf16[4,2,640]{2,1,0:T(2,128)(2,1)} %reshape.193), calls=%async_computation.2 | async-start | bytes 20480 | tf_op jit(solution)/shard_map/all_to_all | solution.py:67
  27.6 5.6 %all-to-all-done.2 = bf16[4,2,640]{2,1,0:T(2,128)(2,1)S(1)} async-done(((bf16[4,2,640]{2,1,0:T(2,128)(2,1)}), bf16[4,2,640]{2,1,0:T(2,128)(2,1)S(1)}, u32[]{:S(2)}, u32[]{:S(2)}) %all-to-all-start.2) | async-done | bytes 10272 | tf_op jit(solution)/shard_map/all_to_all | solution.py:67
  33.2 4.3 %all-to-all-start.1 = ((bf16[160,32,128]{2,1,0:T(8,128)(2,1)}), bf16[160,32,128]{2,1,0:T(8,128)(2,1)}, u32[]{:S(2)}, u32[]{:S(2)}) async-start(bf16[160,32,128]{2,1,0:T(8,128)(2,1)} %param.10), calls=%async_computation.1 | async-start | bytes 2621440 | tf_op jit(solution)/shard_map/all_to_all | solution.py:66
  38.7 11.5 %collective-permute-done.1 = bf16[40,32,256]{2,1,0:T(8,128)(2,1)} collective-permute-done((bf16[40,32,256]{2,1,0:T(8,128)(2,1)}, bf16[40,32,256]{2,1,0:T(8,128)(2,1)}, u32[]{:S(2)}, u32[]{:S(2)}) %collective-permute-start.1) | collective-permute-done | bytes 655392 | tf_op jit(solution)/shard_map/ppermute | solution.py:11
  52.5 11.6 %collective-permute-done.3 = bf16[40,32,256]{2,1,0:T(8,128)(2,1)} collective-permute-done((bf16[40,32,256]{2,1,0:T(8,128)(2,1)}, bf16[40,32,256]{2,1,0:T(8,128)(2,1)}, u32[]{:S(2)}, u32[]{:S(2)}) %collective-permute-start.3) | collective-permute-done | bytes 655392 | tf_op jit(solution)/shard_map/ppermute | solution.py:11
  71.5 5.0 %all-to-all-start = ((bf16[160,32,256]{2,1,0:T(8,128)(2,1)}), bf16[160,32,256]{2,1,0:T(8,128)(2,1)S(1)}, u32[]{:S(2)}, u32[]{:S(2)}) async-start(bf16[160,32,256]{2,1,0:T(8,128)(2,1)} %broadcast_select_fusion.1), calls=%async_computation | async-start | bytes 5242880 | tf_op jit(solution)/shard_map/all_to_all | solution.py:65
  80.7 54.4 %all-to-all-done = bf16[160,32,256]{2,1,0:T(8,128)(2,1)S(1)} async-done(((bf16[160,32,256]{2,1,0:T(8,128)(2,1)}), bf16[160,32,256]{2,1,0:T(8,128)(2,1)S(1)}, u32[]{:S(2)}, u32[]{:S(2)}) %all-to-all-start) | async-done | bytes 2621472 | tf_op jit(solution)/shard_map/all_to_all | solution.py:65
  137.3 6.6 %multiply_convert_fusion = (bf16[40,4,32,256]{3,2,0,1:T(8,128)(2,1)S(1)}, f32[40,4,32,256]{3,2,0,1:T(8,128)}) fusion(f32[40]{0:T(128)S(1)} %dynamic_slice.3, f32[4,32]{1,0:T(4,128)S(1)} %mul.53, f32[4,32,32,1]{1,0,2,3:T(4,128)S(1)} %bitcast.144, f32[40,4,32,256]{3,2,1,0:T(8,128)S(1)} %bitcast.138), kind=kOutput, calls=%fused_computation.10 | convolution fusion | flops 507248640 | bytes 13124256 | tf_op jit(solution)/shard_map/gce,fgck->fgek/dot_general | solution.py:19
  145.9 2.9 copy.35
  148.8 3.7 %fusion.1 = f32[40,128,256]{2,1,0:T(8,128)} fusion(f32[40,4,32,256]{3,2,1,0:T(8,128)S(1)} %copy.35, f32[40]{0:T(128)S(1)} %dynamic_slice.3, f32[128]{0:T(128)S(1)} %sqrt.3), kind=kLoop, calls=%fused_computation.7 | loop fusion | flops 2621440 | bytes 10486432 | tf_op jit(solution)/shard_map/mul | solution.py:77
  152.5 45.5 %all-reduce.4.cloned.1.call-done = f32[256,256]{0,1:T(8,128)} async-done(((f32[256,256]{0,1:T(8,128)}), f32[256,256]{0,1:T(8,128)}) %all-reduce.4.cloned.1.call-update) | async-done | bytes 262160 | tf_op jit(solution)/shard_map/psum | solution.py:85
  198.1 4.4 %fusion.45 = f32[1,256,1]{1,0,2:T(1,128)S(1)} fusion(f32[40,128,256]{2,1,0:T(8,128)} %fusion.1, f32[40,128,1]{1,2,0:T(1,128)S(1)} %copy.43), kind=kOutput, calls=%fused_computation.90 | convolution fusion | flops 15728640 | bytes 5264384 | tf_op jit(solution)/shard_map/fck,fc->k/dot_general | solution.py:80
  202.5 11.8 %psum.30 = f32[256]{0:T(256)S(1)} all-reduce(f32[256]{0:T(256)S(1)} %bitcast.148), channel_id=1, replica_groups=mesh['tile'=8,'chan'=4] {'tile'}, use_global_device_ids=true, to_apply=%region_6.7 | all-reduce | flops 256 | bytes 2048 | tf_op jit(solution)/shard_map/psum | solution.py:85
  214.2 12.2 %psum.31 = f32[256]{0:T(256)S(1)} all-reduce(f32[256]{0:T(256)S(1)} %psum.30), channel_id=1, replica_groups=mesh['tile'=8,'chan'=4] {'chan'}, use_global_device_ids=true, to_apply=%region_7.8 | all-reduce | flops 256 | bytes 2048 | tf_op jit(solution)/shard_map/psum | solution.py:85
  226.5 8.7 %all-reduce.6.cloned.1.call-done = f32[256,256]{0,1:T(8,128)} async-done(((f32[256,256]{0,1:T(8,128)}), f32[256,256]{0,1:T(8,128)}) %all-reduce.6.cloned.1.call-update) | async-done | bytes 262160 | tf_op jit(solution)/shard_map/psum | solution.py:85
  237.3 11.7 %cholesky.49 = f32[128,128]{1,0:T(8,128)S(1)} custom-call(f32[128,128]{1,0:T(8,128)S(1)} %cholesky.115), custom_call_target="Cholesky" | custom-call | tf_op jit(solution)/shard_map/jit(cholesky)/cholesky | solution.py:88
  249.1 9.8 %custom-call.18 = f32[1,128,128]{1,2,0:T(8,128)S(1)} custom-call(f32[1,128,128]{2,1,0:T(8,128)S(1)} %get-tuple-element.36), custom_call_target="InvertDiagBlocksLowerTriangular" | custom-call | tf_op jit(solution)/shard_map/jit(cholesky)/cholesky | solution.py:88
  259.4 11.7 %cholesky.103 = f32[128,128]{1,0:T(8,128)S(1)} custom-call(f32[128,128]{1,0:T(8,128)S(1)} %convolution_subtract_fusion.1), custom_call_target="Cholesky" | custom-call | tf_op jit(solution)/shard_map/jit(cholesky)/cholesky | solution.py:88
  273.6 4.2 %while.1 = (s32[]{:T(128)}, f32[256,256]{0,1:T(8,128)S(1)}, s32[2,2]{1,0:T(2,128)S(1)}, f32[2,128,128]{2,1,0:T(8,128)S(1)}, s32[]{:T(128)}) while((s32[]{:T(128)}, f32[256,256]{0,1:T(8,128)S(1)}, s32[2,2]{1,0:T(2,128)S(1)}, f32[2,128,128]{2,1,0:T(8,128)S(1)}, s32[]{:T(128)}) %tuple.27), condition=%wide.while_cond, body=%wide.while_body.sunk | while | flops 2 | bytes 393321 | solution.py:93
  277.8 19.9 %custom-call.19 = f32[2,128,128]{1,2,0:T(8,128)S(1)} custom-call(f32[2,128,128]{2,1,0:T(8,128)S(1)} %get-tuple-element.12), custom_call_target="InvertDiagBlocksLowerTriangular" | custom-call | tf_op jit(solution)/shard_map/triangular_solve | solution.py:93
  299.7 7.4 %fusion = bf16[12288,256]{0,1:T(8,128)(2,1)} fusion(bf16[12288,256]{1,0:T(8,128)(2,1)} %bitcast.139, f32[128,256]{1,0:T(8,128)S(1)} %fusion.23, f32[128,256]{1,0:T(8,128)S(1)} %fusion.32, f32[256]{0:T(256)S(1)} %bitcast.147), kind=kOutput, calls=%fused_computation.5 | convolution fusion | flops 1614020608 | bytes 12846080 | tf_op jit(solution)/shard_map/dot_general | solution.py:98
  307.1 8.6 %copy.38 = bf16[12288,256]{1,0:T(8,128)(2,1)} copy(bf16[12288,256]{0,1:T(8,128)(2,1)} %fusion) | data formatting | bytes 12582912 | tf_op jit(solution)/shard_map/convert_element_type | solution.py:98
  (98 shorter events, 35.1 us)
Async XLA Ops:
  15.2 6.7 %copy-start.3 = (f32[160,32]{0,1:T(8,128)S(1)}, f32[160,32]{0,1:T(8,128)}, u32[]{:S(2)}) copy-start(f32[160,32]{0,1:T(8,128)} %param.11) | copy-start | bytes 61444
  15.3 12.4 %copy-start.5 = (s32[160]{0:T(256)S(1)}, s32[160]{0:T(256)}, u32[]{:S(2)}) copy-start(s32[160]{0:T(256)} %param.16) | copy-start | bytes 1924
  16.8 20.7 %collective-permute-start = (bf16[40,32,256]{2,1,0:T(8,128)(2,1)}, bf16[40,32,256]{2,1,0:T(8,128)(2,1)}, u32[]{:S(2)}, u32[]{:S(2)}) collective-permute-start(bf16[40,32,256]{2,1,0:T(8,128)(2,1)} %get-tuple-element.34), channel_id=1, source_target_pairs={{0,24},{4,28},{8,0},{12,4},{16,8},{20,12},{24,16},{28,20},{1,25},{... | collective-permute-start | bytes 1966088 | tf_op jit(solution)/shard_map/ppermute | solution.py:11
  20.7 29.5 %collective-permute-start.1 = (bf16[40,32,256]{2,1,0:T(8,128)(2,1)}, bf16[40,32,256]{2,1,0:T(8,128)(2,1)}, u32[]{:S(2)}, u32[]{:S(2)}) collective-permute-start(bf16[40,32,256]{2,1,0:T(8,128)(2,1)} %get-tuple-element.33), channel_id=1, source_target_pairs={{0,28},{4,0},{8,4},{12,8},{16,12},{20,16},{24,20},{28,24},{1,29},{... | collective-permute-start | bytes 1966088 | tf_op jit(solution)/shard_map/ppermute | solution.py:11
  20.7 30.7 %collective-permute-start.2 = (bf16[40,32,256]{2,1,0:T(8,128)(2,1)}, bf16[40,32,256]{2,1,0:T(8,128)(2,1)}, u32[]{:S(2)}, u32[]{:S(2)}) collective-permute-start(bf16[40,32,256]{2,1,0:T(8,128)(2,1)} %get-tuple-element.32), channel_id=1, source_target_pairs={{0,4},{4,8},{8,12},{12,16},{16,20},{20,24},{24,28},{28,0},{1,5},{5... | collective-permute-start | bytes 1966088 | tf_op jit(solution)/shard_map/ppermute | solution.py:11
  21.2 42.9 %collective-permute-start.3 = (bf16[40,32,256]{2,1,0:T(8,128)(2,1)}, bf16[40,32,256]{2,1,0:T(8,128)(2,1)}, u32[]{:S(2)}, u32[]{:S(2)}) collective-permute-start(bf16[40,32,256]{2,1,0:T(8,128)(2,1)} %get-tuple-element.31), channel_id=1, source_target_pairs={{0,8},{4,12},{8,16},{12,20},{16,24},{20,28},{24,0},{28,4},{1,9},{5... | collective-permute-start | bytes 1966088 | tf_op jit(solution)/shard_map/ppermute | solution.py:11
  22.7 10.5 %all-to-all-start.2 = ((bf16[4,2,640]{2,1,0:T(2,128)(2,1)}), bf16[4,2,640]{2,1,0:T(2,128)(2,1)S(1)}, u32[]{:S(2)}, u32[]{:S(2)}) async-start(bf16[4,2,640]{2,1,0:T(2,128)(2,1)} %reshape.193), calls=%async_computation.2 | async-start | bytes 20480 | tf_op jit(solution)/shard_map/all_to_all | solution.py:67
  33.2 38.3 %all-to-all-start.1 = ((bf16[160,32,128]{2,1,0:T(8,128)(2,1)}), bf16[160,32,128]{2,1,0:T(8,128)(2,1)}, u32[]{:S(2)}, u32[]{:S(2)}) async-start(bf16[160,32,128]{2,1,0:T(8,128)(2,1)} %param.10), calls=%async_computation.1 | async-start | bytes 2621440 | tf_op jit(solution)/shard_map/all_to_all | solution.py:66
  65.3 1.7 copy-start.1
  71.5 5.7 %copy-start.6 = (f32[128]{0:T(128)S(1)}, f32[128]{0:T(128)}, u32[]{:S(2)}) copy-start(f32[128]{0:T(128)} %param.13) | copy-start | bytes 1540
  71.5 5.8 %copy-start.4 = (f32[128,32]{0,1:T(8,128)S(1)}, f32[128,32]{0,1:T(8,128)}, u32[]{:S(2)}) copy-start(f32[128,32]{0,1:T(8,128)} %param.12) | copy-start | bytes 49156
  71.5 63.6 %all-to-all-start = ((bf16[160,32,256]{2,1,0:T(8,128)(2,1)}), bf16[160,32,256]{2,1,0:T(8,128)(2,1)S(1)}, u32[]{:S(2)}, u32[]{:S(2)}) async-start(bf16[160,32,256]{2,1,0:T(8,128)(2,1)} %broadcast_select_fusion.1), calls=%async_computation | async-start | bytes 5242880 | tf_op jit(solution)/shard_map/all_to_all | solution.py:65
  76.5 121.5 %all-reduce.4.cloned.1.call-start = ((), (), s32[]{:S(2)}) async-start(), calls=%async_computation.3 | async-start | bytes 524288 | tf_op jit(solution)/shard_map/psum | solution.py:85
  135.1 1.3 copy-start
  145.8 89.4 %all-reduce.6.cloned.1.call-start = ((), (), s32[]{:S(2)}) async-start(), calls=%async_computation.4 | async-start | bytes 524288 | tf_op jit(solution)/shard_map/psum | solution.py:85
  226.5 72.4 %copy-start.2 = (f32[256,256]{1,0:T(8,128)S(1)}, f32[256,256]{1,0:T(8,128)}, u32[]{:S(2)}) copy-start(f32[256,256]{1,0:T(8,128)} %param.14) | copy-start | bytes 786436
Sparse Core Ops, SparseCore 0:
  145.9 52.0 all-reduce.3
  200.4 34.7 all-reduce.5
